TPU v7x, 256 devices: a whole 4x4x8 slice. The times are simulated.
256 devices in a mesh: dp: 16 (over x, y), head: 16 (over z, core).
Axes of the slice: x: 4, y: 4, z: 8, core: 2. Of those that a mesh axis runs over, the one named last changes fastest.
Arguments:
- latents: bfloat16 [2048, 512], P('dp'), may hold values from -6 to 6
- targets: bfloat16 [2048, 32768], P('dp', 'head'), may hold values from -6 to 6
- kv_weight: bfloat16 [512, 32768], P(None, 'head'), may hold values from -0.25 to 0.25
- momentum: float32 [512, 16, 2048], P(None, 'head', 'dp'), may hold values from -120 to 120
Outputs:
- momentum_out: float32 [512, 16, 2048], P(None, 'head', 'dp')
- update: float32 [512, 16, 2048], P(None, 'head', 'dp')
All inputs are finite; a program needn't handle non-finite values.
Results may differ from a plain program's by a relative error of at most 0.0003.
The roundings to bfloat16 on the way count: a program that leaves them out, or rounds other values in their place, can miss the bound.
Values may be sent and summed in bfloat16 or wider, within the bound.
A program may use at most 64 MiB of HBM per device.

v0:
```python
import math
import jax
import jax.numpy as jnp
from jax import lax
from jax.sharding import PartitionSpec as P

C = 32768
decay_rate = 0.95
linear_coef = 3.4445
square_coef = -4.775
quint_coef = 2.0315
epsilon = 1e-07
HIGHEST = lax.Precision.HIGHEST


def local(latents, targets, kv_weight, momentum):
    latent_width = momentum.shape[0]
    sub_width = momentum.shape[2]
    total_tokens = latents.shape[0] * lax.axis_size("dp")
    all_latents = lax.all_gather(latents, "dp", axis=0, tiled=True)
    my_targets = lax.all_to_all(targets, "dp", split_axis=1, concat_axis=0, tiled=True)
    start = lax.axis_index("dp") * sub_width
    my_weight = lax.dynamic_slice(kv_weight, (0, start), (latent_width, sub_width))
    residual = (
        jnp.dot(all_latents, my_weight, preferred_element_type=jnp.float32)
        - my_targets.astype(jnp.float32)
    ).astype(jnp.bfloat16)
    gradient = lax.dot_general(
        all_latents, residual, (((0,), (0,)), ((), ())), preferred_element_type=jnp.float32
    ) * (1.0 / math.sqrt(total_tokens))
    momentum_new = decay_rate * momentum.reshape(latent_width, sub_width) + gradient
    nesterov = gradient + decay_rate * momentum_new
    gram = lax.psum(
        lax.dot_general(nesterov, nesterov, (((1,), (1,)), ((), ())), precision=HIGHEST),
        ("dp", "head"),
    )
    inverse = 1.0 / (jnp.sqrt(jnp.trace(gram)) + epsilon)
    gram = gram * (inverse * inverse)
    eye = jnp.eye(latent_width, dtype=jnp.float32)
    first = (
        linear_coef * eye + square_coef * gram + quint_coef * jnp.dot(gram, gram, precision=HIGHEST)
    )
    second_gram = jnp.dot(first, jnp.dot(gram, first, precision=HIGHEST), precision=HIGHEST)
    second = (
        linear_coef * eye
        + square_coef * second_gram
        + quint_coef * jnp.dot(second_gram, second_gram, precision=HIGHEST)
    )
    iterate = jnp.dot(first, nesterov * (inverse * math.sqrt(C)), precision=HIGHEST)
    update = jnp.dot(second, iterate, precision=HIGHEST)
    return (
        momentum_new.reshape(latent_width, 1, sub_width),
        update.reshape(latent_width, 1, sub_width),
    )


def solution(mesh):
    return jax.shard_map(
        local,
        mesh=mesh,
        in_specs=(P("dp", None), P("dp", "head"), P(None, "head"), P(None, "head", "dp")),
        out_specs=(P(None, "head", "dp"), P(None, "head", "dp")),
        check_vma=False,
    )
```

profile of v0, /device:TPU:2, one launch (start us, length us, event | category | flops | bytes accessed | tf_op | source)
XLA Modules:
  0.0 346.6 jit_solution(12459691134939242747)
XLA Ops:
  7.2 0.0 copy-start
  7.2 0.0 copy-start.2
  7.2 0.0 all-gather.2.cloned.1.call-start
  7.2 0.7 all-gather.2.cloned.1.call-update
  7.9 2.0 copy.13
  10.0 7.5 %all-to-all-start = ((bf16[128,16,128]{0,2,1:T(8,128)(2,1)}), bf16[128,16,128]{0,2,1:T(8,128)(2,1)}, u32[]{:S(2)}, u32[]{:S(2)}) async-start(bf16[128,16,128]{0,2,1:T(8,128)(2,1)} %bitcast.2), calls=%async_computation | async-start | bytes 1048576 | tf_op jit(solution)/shard_map/all_to_all | solution.py:21
  17.5 0.0 all-reduce.2.cloned.1.call-start
  17.5 0.0 copy-done.2
  17.5 0.1 copy.12
  17.6 9.2 %all-to-all-done = bf16[128,16,128]{0,2,1:T(8,128)(2,1)} async-done(((bf16[128,16,128]{0,2,1:T(8,128)(2,1)}), bf16[128,16,128]{0,2,1:T(8,128)(2,1)}, u32[]{:S(2)}, u32[]{:S(2)}) %all-to-all-start) | async-done | bytes 524320 | tf_op jit(solution)/shard_map/all_to_all | solution.py:21
  26.9 1.1 convert_bitcast_fusion
  28.0 1.3 copy.14
  29.3 2.6 copy.15
  31.9 31.2 %all-gather.2.cloned.1.call-done = bf16[2048,512]{1,0:T(8,128)(2,1)} async-done(((bf16[128,512]{1,0:T(8,128)(2,1)}), bf16[2048,512]{1,0:T(8,128)(2,1)}) %all-gather.2.cloned.1.call-update) | async-done | bytes 2097168 | tf_op jit(solution)/shard_map/all_gather | solution.py:20
  63.1 0.0 copy-done
  63.1 3.7 %fusion.6 = f32[512,128]{0,1:T(8,128)S(1)} fusion(bf16[2048,512]{1,0:T(8,128)(2,1)} %all-gather.2.cloned.1.call-done, f32[2048,128]{0,1:T(8,128)} %copy.15, bf16[512,2048]{1,0:T(8,128)(2,1)S(1)} %copy-done, s32[]{:T(128)S(6)} %select_n.8), kind=kOutput, calls=%fused_computation.11 | convolution fusion | flops 537460736 | bytes 5636100 | tf_op jit(solution)/shard_map/dot_general | solution.py:28
  66.7 2.1 fusion.18
  68.8 0.0 all-reduce.2.cloned.1.call-update
  68.9 0.8 copy.16
  69.7 255.0 %all-reduce.2.cloned.1.call-done = f32[512,512]{1,0:T(8,128)} async-done(((f32[512,512]{1,0:T(8,128)}), f32[512,512]{1,0:T(8,128)}) %all-reduce.2.cloned.1.call-update) | async-done | bytes 1048592 | tf_op jit(solution)/shard_map/psum | solution.py:33
  324.7 1.9 select_reduce_fusion
  327.3 0.0 copy-start.1
  327.4 4.1 %fusion.3 = f32[512,512]{1,0:T(8,128)S(1)} fusion(f32[512,512]{1,0:T(8,128)} %all-reduce.2.cloned.1.call-done, f32[]{:T(128)S(6)} %mul.65), kind=kOutput, calls=%fused_computation.8 | convolution fusion | flops 1612709888 | bytes 2097156 | tf_op jit(solution)/shard_map/dot_general | solution.py:41
  331.4 1.0 fusion.12
  332.4 0.0 copy-done.1
  332.4 1.9 fusion.8
  334.3 1.8 fusion.23
  336.2 1.9 fusion.2
  338.1 1.7 fusion.24
  (1 shorter events, 0.0 us)
Async XLA Ops:
  7.2 55.9 %copy-start = (bf16[512,2048]{1,0:T(8,128)(2,1)S(1)}, bf16[512,2048]{1,0:T(8,128)(2,1)}, u32[]{:S(2)}) copy-start(bf16[512,2048]{1,0:T(8,128)(2,1)} %param.6) | copy-start | bytes 6291460
  7.2 10.3 %copy-start.2 = (f32[512,1,128]{2,1,0:T(1,128)S(1)}, f32[512,1,128]{2,1,0:T(1,128)}, u32[]{:S(2)}) copy-start(f32[512,1,128]{2,1,0:T(1,128)} %param.7) | copy-start | bytes 786436
  7.2 55.9 %all-gather.2.cloned.1.call-start = ((), (), s32[]{:S(2)}) async-start(), calls=%async_computation.1 | async-start | bytes 2228224 | tf_op jit(solution)/shard_map/all_gather | solution.py:20
  10.0 16.9 %all-to-all-start = ((bf16[128,16,128]{0,2,1:T(8,128)(2,1)}), bf16[128,16,128]{0,2,1:T(8,128)(2,1)}, u32[]{:S(2)}, u32[]{:S(2)}) async-start(bf16[128,16,128]{0,2,1:T(8,128)(2,1)} %bitcast.2), calls=%async_computation | async-start | bytes 1048576 | tf_op jit(solution)/shard_map/all_to_all | solution.py:21
  17.5 307.3 %all-reduce.2.cloned.1.call-start = ((), (), s32[]{:S(2)}) async-start(), calls=%async_computation.2 | async-start | bytes 2097152 | tf_op jit(solution)/shard_map/psum | solution.py:33
  327.3 5.1 %copy-start.1 = (f32[512,512]{1,0:T(8,128)S(1)}, f32[512,512]{1,0:T(8,128)}, u32[]{:S(2)}) copy-start(f32[512,512]{1,0:T(8,128)} %all-reduce.2.cloned.1.call-done) | copy-start | bytes 3145732
Sparse Core Ops, SparseCore 0:
  10.5 52.5 all-gather.1
  68.9 255.7 all-reduce.1
where the time goes:
time: 347 us
  waiting for transfers between devices  296 us (85%)
  matrix products  18.1 us (5%)
  between operations  14.9 us (4%)
  starting transfers between devices  7.55 us (2%)
  local copies, waits for them, and re-layouts  6.9 us (2%)
    psum x1, waiting for transfers between devices, local(): lax.psum(lax.dot_general(nesterov, nesterov, (((1,), (1,)), ((), ())), pr...  255 us
    all_gather x1, waiting for transfers between devices, local(): all_latents = lax.all_gather(latents, 'dp', axis=0, tiled=True)  31.2 us
    all_to_all x1, waiting for transfers between devices, local(): lax.all_to_all(targets, 'dp', split_axis=1, concat_axis=0, tiled=True)  9.24 us
    all_to_all x1, starting transfers between devices, local(): lax.all_to_all(targets, 'dp', split_axis=1, concat_axis=0, tiled=True)  7.48 us
  transfers between devices with their start and end apart: 3, of which 3 were waited for; matrix products, arithmetic and copies ran while one was open for 2% of the time, Pallas kernels for 0%

commit v1 on v0

--- a/solution.py
+++ b/solution.py
@@ -11,6 +11,11 @@
 quint_coef = 2.0315
 epsilon = 1e-07
 HIGHEST = lax.Precision.HIGHEST
+
+
+def axis_by_axis(value, inner_axis, outer_axis):
+    inner = lax.psum(value, inner_axis)
+    return lax.psum(inner, outer_axis)
 
 
 def local(latents, targets, kv_weight, momentum):
@@ -30,9 +35,10 @@
     ) * (1.0 / math.sqrt(total_tokens))
     momentum_new = decay_rate * momentum.reshape(latent_width, sub_width) + gradient
     nesterov = gradient + decay_rate * momentum_new
-    gram = lax.psum(
+    gram = axis_by_axis(
         lax.dot_general(nesterov, nesterov, (((1,), (1,)), ((), ())), precision=HIGHEST),
-        ("dp", "head"),
+        "head",
+        "dp",
     )
     inverse = 1.0 / (jnp.sqrt(jnp.trace(gram)) + epsilon)
     gram = gram * (inverse * inverse)

time: 347 us -> 305 us (0.88)
  waiting for transfers between devices: 296 us -> 252 us
    psum x1 -> x2, waiting for transfers between devices: 255 us -> 211 us  [the longest x1 111 us: axis_by_axis(): inner = lax.psum(value, inner_axis)]
  transfers between devices with their start and end apart: 3 -> 4, of which waited for: 3 -> 4; matrix products, arithmetic and copies ran while one was open for 2% -> 3% of each run, Pallas kernels for 0% -> 0%
where the time goes in v1:
time: 305 us; the launch traced here: 304 us
  waiting for transfers between devices  252 us (83%)
  matrix products  20 us (7%)
  between operations  14.6 us (5%)
  starting transfers between devices  7.78 us (3%)
  local copies, waits for them, and re-layouts  6.92 us (2%)
  other arithmetic  3.13 us (1%)
    psum x1, waiting for transfers between devices, axis_by_axis(): inner = lax.psum(value, inner_axis)  111 us
    psum x1, waiting for transfers between devices, axis_by_axis(): return lax.psum(inner, outer_axis)  99.6 us
    all_gather x1, waiting for transfers between devices, local(): all_latents = lax.all_gather(latents, 'dp', axis=0, tiled=True)  31.2 us
    all_to_all x1, waiting for transfers between devices, local(): lax.all_to_all(targets, 'dp', split_axis=1, concat_axis=0, tiled=True)  9.22 us
    all_to_all x1, starting transfers between devices, local(): lax.all_to_all(targets, 'dp', split_axis=1, concat_axis=0, tiled=True)  7.48 us
  transfers between devices with their start and end apart: 4, of which 4 were waited for; matrix products, arithmetic and copies ran while one was open for 3% of the time, Pallas kernels for 0%

profile of v1, /device:TPU:2, one launch (start us, length us, event | category | flops | bytes accessed | tf_op | source)
XLA Modules:
  0.0 304.4 jit_solution(3524235866132822471)
XLA Ops:
  7.2 0.0 copy-start
  7.2 0.0 copy-start.4
  7.2 0.0 all-gather.2.cloned.1.call-start
  7.2 0.7 all-gather.2.cloned.1.call-update
  7.9 2.1 copy.13
  10.0 7.5 %all-to-all-start = ((bf16[128,16,128]{0,2,1:T(8,128)(2,1)}), bf16[128,16,128]{0,2,1:T(8,128)(2,1)}, u32[]{:S(2)}, u32[]{:S(2)}) async-start(bf16[128,16,128]{0,2,1:T(8,128)(2,1)} %bitcast.2), calls=%async_computation | async-start | bytes 1048576 | tf_op jit(solution)/shard_map/all_to_all | solution.py:26
  17.5 0.0 all-reduce.3.cloned.1.call-start
  17.5 0.0 copy-done.4
  17.5 0.1 copy.12
  17.7 0.0 copy-start.3
  17.7 9.2 %all-to-all-done = bf16[128,16,128]{0,2,1:T(8,128)(2,1)} async-done(((bf16[128,16,128]{0,2,1:T(8,128)(2,1)}), bf16[128,16,128]{0,2,1:T(8,128)(2,1)}, u32[]{:S(2)}, u32[]{:S(2)}) %all-to-all-start) | async-done | bytes 524320 | tf_op jit(solution)/shard_map/all_to_all | solution.py:26
  26.9 1.1 convert_bitcast_fusion
  28.0 1.3 copy.14
  29.4 2.5 copy.15
  31.9 31.2 %all-gather.2.cloned.1.call-done = bf16[2048,512]{1,0:T(8,128)(2,1)} async-done(((bf16[128,512]{1,0:T(8,128)(2,1)}), bf16[2048,512]{1,0:T(8,128)(2,1)}) %all-gather.2.cloned.1.call-update) | async-done | bytes 2097168 | tf_op jit(solution)/shard_map/all_gather | solution.py:25
  63.1 0.0 copy-done
  63.1 3.7 %fusion.6 = f32[512,128]{0,1:T(8,128)S(1)} fusion(bf16[2048,512]{1,0:T(8,128)(2,1)} %all-gather.2.cloned.1.call-done, f32[2048,128]{0,1:T(8,128)} %copy.15, bf16[512,2048]{1,0:T(8,128)(2,1)S(1)} %copy-done, s32[]{:T(128)S(6)} %select_n.8), kind=kOutput, calls=%fused_computation.11 | convolution fusion | flops 537460736 | bytes 5636100 | tf_op jit(solution)/shard_map/dot_general | solution.py:33
  66.7 2.0 fusion.18
  68.8 0.0 all-reduce.3.cloned.1.call-update
  68.8 0.2 all-reduce.5.cloned.1.call-start
  69.0 111.2 %all-reduce.3.cloned.1.call-done = f32[512,512]{1,0:T(8,128)} async-done(((f32[512,512]{1,0:T(8,128)}), f32[512,512]{1,0:T(8,128)}) %all-reduce.3.cloned.1.call-update) | async-done | bytes 1048592 | tf_op jit(solution)/shard_map/psum | solution.py:17
  180.2 0.0 all-reduce.5.cloned.1.call-update
  180.2 0.0 copy-done.3
  180.3 0.8 copy.16
  181.1 99.6 %all-reduce.5.cloned.1.call-done = f32[512,512]{1,0:T(8,128)} async-done(((f32[512,512]{1,0:T(8,128)}), f32[512,512]{1,0:T(8,128)}) %all-reduce.5.cloned.1.call-update) | async-done | bytes 1048592 | tf_op jit(solution)/shard_map/psum | solution.py:18
  280.7 2.0 select_reduce_fusion
  283.4 0.0 copy-start.2
  283.4 4.1 %fusion.3 = f32[512,512]{1,0:T(8,128)S(1)} fusion(f32[512,512]{1,0:T(8,128)} %all-reduce.5.cloned.1.call-done, f32[]{:T(128)S(6)} %mul.65), kind=kOutput, calls=%fused_computation.8 | convolution fusion | flops 1612709888 | bytes 2097156 | tf_op jit(solution)/shard_map/dot_general | solution.py:47
  287.5 0.0 copy-done.2
  287.5 1.9 fusion.8
  289.4 1.8 fusion.23
  291.2 2.9 fusion.2
  294.1 0.0 copy-start.1
  294.1 2.0 fusion.12
  296.1 0.0 copy-done.1
  296.1 1.7 fusion.24
  (1 shorter events, 0.0 us)
Async XLA Ops:
  7.2 55.9 %copy-start = (bf16[512,2048]{1,0:T(8,128)(2,1)S(1)}, bf16[512,2048]{1,0:T(8,128)(2,1)}, u32[]{:S(2)}) copy-start(bf16[512,2048]{1,0:T(8,128)(2,1)} %param.6) | copy-start | bytes 6291460
  7.2 10.3 %copy-start.4 = (f32[512,1,128]{2,1,0:T(1,128)S(1)}, f32[512,1,128]{2,1,0:T(1,128)}, u32[]{:S(2)}) copy-start(f32[512,1,128]{2,1,0:T(1,128)} %param.7) | copy-start | bytes 786436
  7.2 55.9 %all-gather.2.cloned.1.call-start = ((), (), s32[]{:S(2)}) async-start(), calls=%async_computation.1 | async-start | bytes 2228224 | tf_op jit(solution)/shard_map/all_gather | solution.py:25
  10.0 16.9 %all-to-all-start = ((bf16[128,16,128]{0,2,1:T(8,128)(2,1)}), bf16[128,16,128]{0,2,1:T(8,128)(2,1)}, u32[]{:S(2)}, u32[]{:S(2)}) async-start(bf16[128,16,128]{0,2,1:T(8,128)(2,1)} %bitcast.2), calls=%async_computation | async-start | bytes 1048576 | tf_op jit(solution)/shard_map/all_to_all | solution.py:26
  17.5 162.7 %all-reduce.3.cloned.1.call-start = ((), (), s32[]{:S(2)}) async-start(), calls=%async_computation.2 | async-start | bytes 2097152 | tf_op jit(solution)/shard_map/psum | solution.py:17
  17.7 162.6 %copy-start.3 = (f32[512,1,128]{0,2,1:T(8,128)}, f32[512,1,128]{0,2,1:T(8,128)S(1)}, u32[]{:S(2)}) copy-start(f32[512,1,128]{0,2,1:T(8,128)S(1)} %copy.12) | copy-start | bytes 786436
  68.8 212.0 %all-reduce.5.cloned.1.call-start = ((), (), s32[]{:S(2)}) async-start(), calls=%async_computation.3 | async-start | bytes 2097152 | tf_op jit(solution)/shard_map/psum | solution.py:18
  283.4 4.1 %copy-start.2 = (f32[512,512]{1,0:T(8,128)S(1)}, f32[512,512]{1,0:T(8,128)}, u32[]{:S(2)}) copy-start(f32[512,512]{1,0:T(8,128)} %all-reduce.5.cloned.1.call-done) | copy-start | bytes 3145732
  294.1 2.0 copy-start.1
Sparse Core Ops, SparseCore 0:
  10.5 52.5 all-gather.1
  68.9 111.2 all-reduce.2
  183.8 96.9 all-reduce.4
